TPU v7x, 256 devices: a whole 4x4x8 slice. The times are simulated.
256 devices in a mesh: task: 8 (over z_hi, core), row: 8 (over x, z_lo), col: 4 (over y).
Axes of the slice: x: 4, y: 4, z: 8 (z_hi: 4, z_lo: 2; z = z_hi * 2 + z_lo), core: 2. Of those that a mesh axis runs over, the one named last changes fastest.
Arguments:
- activations: bfloat16 [8, 512, 13824], P('task', 'col', 'row'), may hold values from -6 to 6
- weights: bfloat16 [8, 13824, 5120], P('task', 'row', 'col'), may hold values from -0.0625 to 0.0625
- labels: int32 [8, 512], P('task'), may hold values from 0 to 127
- prototypes: bfloat16 [8, 128, 5120], P('task', None, 'col'), may hold values from -6 to 6
Outputs:
- merged: bfloat16 [13824, 5120], P('row', 'col')
- merged_out: bfloat16 [8, 512, 5120], P('task', 'row', 'col')
All inputs are finite; a program needn't handle non-finite values.
Results may differ from a plain program's by a relative error of at most 0.02.
Values may be sent and summed in bfloat16 or wider, within the bound.
A program may use at most 128 MiB of HBM per device.

v0:
```python
import jax
import jax.numpy as jnp
from jax import lax
from jax.sharding import PartitionSpec as P


def class_targets(label_rows, protos):
    count = label_rows.shape[0]
    onehot = (
        label_rows[:, None] == lax.broadcasted_iota(jnp.int32, (count, protos.shape[0]), 1)
    ).astype(jnp.bfloat16)
    return jnp.dot(onehot, protos, preferred_element_type=jnp.float32)


def local(activations, weights, labels, prototypes):
    acts = activations[0]
    weight = weights[0]
    label_row = labels[0]
    protos = prototypes[0]
    full_acts = lax.all_gather(acts, "col", axis=0, tiled=True)
    partial_out = jnp.dot(full_acts, weight, preferred_element_type=jnp.float32)
    output = lax.psum(partial_out.astype(jnp.bfloat16), "row").astype(jnp.float32)
    grad = output - class_targets(label_row, protos)
    gsq = (grad * grad).astype(jnp.bfloat16)
    wide = full_acts.astype(jnp.float32)
    asq = (wide * wide).astype(jnp.bfloat16)
    fisher = lax.dot_general(asq, gsq, (((0,), (0,)), ((), ())), preferred_element_type=jnp.float32)
    weighted = fisher * weight.astype(jnp.float32)
    numer, denom = (
        lax.psum_scatter(weighted, "task", scatter_dimension=0, tiled=True),
        lax.psum_scatter(fisher, "task", scatter_dimension=0, tiled=True),
    )
    piece = (numer / (denom + 1e-06)).astype(jnp.bfloat16)
    merged = lax.all_gather(piece, "task", axis=0, tiled=True)
    result = lax.psum_scatter(
        jnp.dot(full_acts, merged, preferred_element_type=jnp.float32).astype(jnp.bfloat16),
        "row",
        scatter_dimension=0,
        tiled=True,
    )
    return (merged, result[None])


def solution(mesh):
    placed = (
        P("task", "col", "row"),
        P("task", "row", "col"),
        P("task", None),
        P("task", None, "col"),
    )
    return jax.shard_map(
        local,
        mesh=mesh,
        in_specs=placed,
        out_specs=(P("row", "col"), P("task", "row", "col")),
        check_vma=False,
    )
```

profile of v0, /device:TPU:8, one launch (start us, length us, event | category | flops | bytes accessed | tf_op | source)
XLA Modules:
  0.0 475.8 jit_solution(1805810077636972893)
XLA Ops:
  7.2 0.0 copy-start
  7.2 0.0 all-gather.6.cloned.1.call-start
  7.2 0.7 all-gather.6.cloned.1.call-update
  7.9 0.0 copy-start.2
  7.9 0.0 all-reduce.2.cloned.1.call-start
  8.0 38.4 %all-gather.6.cloned.1.call-done = bf16[1,512,1728]{1,2,0:T(8,128)(2,1)} async-done(((bf16[1,128,1728]{1,2,0:T(8,128)(2,1)}), bf16[1,512,1728]{1,2,0:T(8,128)(2,1)}) %all-gather.6.cloned.1.call-update) | async-done | bytes 1769488 | tf_op jit(solution)/shard_map/all_gather | solution.py:20
  46.4 0.0 copy-start.1
  46.4 6.6 %fusion.4 = bf16[512,1280]{1,0:T(8,128)(2,1)} fusion(bf16[1,1728,1280]{2,1,0:T(8,128)(2,1)} %param.5, bf16[1,512,1728]{1,2,0:T(8,128)(2,1)} %all-gather.6.cloned.1.call-done), kind=kOutput, calls=%fused_computation.7 | convolution fusion | flops 2265579520 | bytes 7503872 | tf_op jit(solution)/shard_map/dot_general | solution.py:21
  53.0 0.0 all-reduce.2.cloned.1.call-update
  53.0 0.0 reduce-scatter.6.cloned.1.call-start
  53.1 90.5 %all-reduce.2.cloned.1.call-done = bf16[512,1280]{1,0:T(8,128)(2,1)} async-done(((bf16[512,1280]{1,0:T(8,128)(2,1)}), bf16[512,1280]{1,0:T(8,128)(2,1)}) %all-reduce.2.cloned.1.call-update) | async-done | bytes 1310736 | tf_op jit(solution)/shard_map/psum | solution.py:22
  143.6 0.0 copy-done
  143.6 0.0 copy-done.2
  143.6 0.0 copy-done.1
  143.6 9.8 %convert_multiply_fusion = (f32[1728,1280]{1,0:T(8,128)}, f32[1728,1280]{1,0:T(8,128)}) fusion(bf16[1,1728,1280]{2,1,0:T(8,128)(2,1)} %param.5, bf16[512,1280]{1,0:T(8,128)(2,1)} %all-reduce.2.cloned.1.call-done, bf16[1,128,1280]{2,1,0:T(8,128)(2,1)S(1)} %copy-done, s32[512]{0:T(512)S(1)} %bitcast.30, bf16[1,512,1728]{1,2,0:T(8,128)(2,1)S(1)} %copy-done.1), kind=kOutput, calls=%fused_computation | convolution fusion | flops 2442461184 | bytes 25528320 | tf_op jit(solution)/shard_map/dot_general | solution.py:27
  153.4 0.0 reduce-scatter.6.cloned.1.call-update
  153.4 0.0 reduce-scatter.8.cloned.1.call-start
  153.4 0.5 reduce-scatter.8.cloned.1.call-update
  154.0 0.0 all-gather.4.cloned.1.call-start
  154.0 96.8 %reduce-scatter.6.cloned.1.call-done = f32[216,1280]{1,0:T(8,128)} async-done(((f32[1728,1280]{1,0:T(8,128)}), f32[216,1280]{1,0:T(8,128)}) %reduce-scatter.6.cloned.1.call-update) | async-done | bytes 1105936 | tf_op jit(solution)/shard_map/reduce_scatter | solution.py:30
  250.8 104.8 %reduce-scatter.8.cloned.1.call-done = f32[216,1280]{1,0:T(8,128)} async-done(((f32[1728,1280]{1,0:T(8,128)}), f32[216,1280]{1,0:T(8,128)}) %reduce-scatter.8.cloned.1.call-update) | async-done | bytes 1105936 | tf_op jit(solution)/shard_map/reduce_scatter | solution.py:31
  355.7 2.5 divide_convert_fusion
  358.2 0.0 all-gather.4.cloned.1.call-update
  358.2 0.0 reduce-scatter.10.cloned.1.call-start
  358.3 54.9 %all-gather.4.cloned.1.call-done = bf16[1728,1280]{1,0:T(8,128)(2,1)} async-done(((bf16[216,1280]{1,0:T(8,128)(2,1)}), bf16[1728,1280]{1,0:T(8,128)(2,1)}) %all-gather.4.cloned.1.call-update) | async-done | bytes 4423696 | tf_op jit(solution)/shard_map/all_gather | solution.py:34
  413.1 4.8 %fusion.7 = bf16[512,1280]{0,1:T(8,128)(2,1)S(1)} fusion(bf16[1728,1280]{1,0:T(8,128)(2,1)} %all-gather.4.cloned.1.call-done, bf16[1,512,1728]{1,2,0:T(8,128)(2,1)S(1)} %copy-done.1), kind=kOutput, calls=%fused_computation.9 | convolution fusion | flops 2265579520 | bytes 7503872 | tf_op jit(solution)/shard_map/dot_general | solution.py:36
  418.0 1.4 copy.8
  419.4 0.0 reduce-scatter.10.cloned.1.call-update
  419.4 42.9 %reduce-scatter.10.cloned.1.call-done = bf16[64,1280]{1,0:T(8,128)(2,1)} async-done(((bf16[512,1280]{1,0:T(8,128)(2,1)}), bf16[64,1280]{1,0:T(8,128)(2,1)}) %reduce-scatter.10.cloned.1.call-update) | async-done | bytes 163856
  462.4 1.1 copy.9
  463.5 0.8 copy.7
  464.3 4.6 copy.12
Async XLA Ops:
  7.2 136.4 %copy-start = (bf16[1,128,1280]{2,1,0:T(8,128)(2,1)S(1)}, bf16[1,128,1280]{2,1,0:T(8,128)(2,1)}, u32[]{:S(2)}) copy-start(bf16[1,128,1280]{2,1,0:T(8,128)(2,1)} %param.7) | copy-start | bytes 983044
  7.2 39.2 %all-gather.6.cloned.1.call-start = ((), (), s32[]{:S(2)}) async-start(), calls=%async_computation.7 | async-start | bytes 2211840 | tf_op jit(solution)/shard_map/all_gather | solution.py:20
  7.9 135.7 %copy-start.2 = (s32[1,512]{1,0:T(1,128)S(1)}, s32[1,512]{1,0:T(1,128)}, u32[]{:S(2)}) copy-start(s32[1,512]{1,0:T(1,128)} %param.6) | copy-start | bytes 6148
  7.9 135.7 %all-reduce.2.cloned.1.call-start = ((), (), s32[]{:S(2)}) async-start(), calls=%async_computation.3 | async-start | bytes 2621440 | tf_op jit(solution)/shard_map/psum | solution.py:22
  46.4 97.2 %copy-start.1 = (bf16[1,512,1728]{1,2,0:T(8,128)(2,1)S(1)}, bf16[1,512,1728]{1,2,0:T(8,128)(2,1)}, u32[]{:S(2)}) copy-start(bf16[1,512,1728]{1,2,0:T(8,128)(2,1)} %all-gather.6.cloned.1.call-done) | copy-start | bytes 5308420
  53.0 197.8 %reduce-scatter.6.cloned.1.call-start = ((), (), s32[]{:S(2)}) async-start(), calls=%async_computation.4 | async-start | bytes 9953280 | tf_op jit(solution)/shard_map/reduce_scatter | solution.py:30
  153.4 202.3 %reduce-scatter.8.cloned.1.call-start = ((), (), s32[]{:S(2)}) async-start(), calls=%async_computation.5 | async-start | bytes 9953280 | tf_op jit(solution)/shard_map/reduce_scatter | solution.py:31
  154.0 259.2 %all-gather.4.cloned.1.call-start = ((), (), s32[]{:S(2)}) async-start(), calls=%async_computation.6 | async-start | bytes 4976640 | tf_op jit(solution)/shard_map/all_gather | solution.py:34
  358.2 104.1 %reduce-scatter.10.cloned.1.call-start = ((), (), s32[]{:S(2)}) async-start(), calls=%async_computation.8 | async-start | bytes 1474560
Sparse Core Ops, SparseCore 0:
  9.8 36.5 all-gather.5
  53.1 90.4 all-reduce.1
  153.5 97.2 reduce-scatter.5
  253.4 102.1 reduce-scatter.7
  358.3 54.7 all-gather.3
  419.6 42.7 reduce-scatter.9
where the time goes:
time: 476 us
  waiting for transfers between devices  430 us (90%)
  matrix products  21.2 us (4%)
  between operations  14.1 us (3%)
  local copies, waits for them, and re-layouts  8.06 us (2%)
    reduce_scatter x1, waiting for transfers between devices, local(): lax.psum_scatter(fisher, 'task', scatter_dimension=0, tiled=True)  105 us
    reduce_scatter x1, waiting for transfers between devices, local(): lax.psum_scatter(weighted, 'task', scatter_dimension=0, tiled=True)  96.8 us
    psum x1, waiting for transfers between devices, local(): lax.psum(partial_out.astype(jnp.bfloat16), 'row').astype(jnp.float32)  90.5 us
    all_gather x1, waiting for transfers between devices, local(): merged = lax.all_gather(piece, 'task', axis=0, tiled=True)  54.9 us
    unnamed x7, waiting for transfers between devices  44.2 us
    all_gather x1, waiting for transfers between devices, local(): full_acts = lax.all_gather(acts, 'col', axis=0, tiled=True)  38.4 us
    dot_general x1, matrix products, local(): lax.dot_general(asq, gsq, (((0,), (0,)), ((), ())), preferred_element_typ...  9.77 us
  transfers between devices with their start and end apart: 6, of which 6 were waited for; matrix products, arithmetic and copies ran while one was open for 0% of the time, Pallas kernels for 0%

commit v1 on v0

--- a/solution.py
+++ b/solution.py
@@ -17,7 +17,14 @@
     weight = weights[0]
     label_row = labels[0]
     protos = prototypes[0]
-    full_acts = lax.all_gather(acts, "col", axis=0, tiled=True)
+    count_2 = lax.axis_size("col")
+    forward = [(i, (i + 1) % count_2) for i in range(count_2)]
+    terms = [acts]
+    for reach in range(1, count_2):
+        terms = [lax.ppermute(terms[0], "col", forward), *terms]
+    whole = jnp.concatenate(terms, axis=0)
+    places = (lax.axis_index("col") + 1) * terms[-1].shape[0]
+    full_acts = jnp.roll(whole, places, axis=0)
     partial_out = jnp.dot(full_acts, weight, preferred_element_type=jnp.float32)
     output = lax.psum(partial_out.astype(jnp.bfloat16), "row").astype(jnp.float32)
     grad = output - class_targets(label_row, protos)

time: 476 us -> 472 us (level)
  waiting for transfers between devices: 430 us -> 421 us
  starting transfers between devices: 0.24 us -> 5.2 us
    unnamed x7 -> x5, waiting for transfers between devices: 44.2 us -> 0.75 us
    reduce_scatter x0 -> x1, waiting for transfers between devices: none -> 42.9 us  [local(): lax.psum_scatter(jnp.dot(full_acts, merged, preferred_element_type=jnp.fl...]
    all_gather x1 -> x0, waiting for transfers between devices: 38.4 us -> none  [local(): full_acts = lax.all_gather(acts, 'col', axis=0, tiled=True)]
    ppermute x0 -> x3, waiting for transfers between devices: none -> 28 us  [local(): terms = [lax.ppermute(terms[0], 'col', forward), *terms]]
    ppermute x0 -> x3, starting transfers between devices: none -> 5 us  [local(): terms = [lax.ppermute(terms[0], 'col', forward), *terms]]
  transfers between devices with their start and end apart: 6 -> 8, of which waited for: 6 -> 8; matrix products, arithmetic and copies ran while one was open for 0% -> 0% of each run, Pallas kernels for 0% -> 0%
where the time goes in v1:
time: 472 us
  waiting for transfers between devices  421 us (89%)
  matrix products  20.6 us (4%)
  between operations  13.9 us (3%)
  local copies, waits for them, and re-layouts  8.61 us (2%)
  starting transfers between devices  5.2 us (1%)
    reduce_scatter x1, waiting for transfers between devices, local(): lax.psum_scatter(fisher, 'task', scatter_dimension=0, tiled=True)  104 us
    reduce_scatter x1, waiting for transfers between devices, local(): lax.psum_scatter(weighted, 'task', scatter_dimension=0, tiled=True)  96.2 us
    psum x1, waiting for transfers between devices, local(): lax.psum(partial_out.astype(jnp.bfloat16), 'row').astype(jnp.float32)  92.9 us
    all_gather x1, waiting for transfers between devices, local(): merged = lax.all_gather(piece, 'task', axis=0, tiled=True)  57.2 us
    reduce_scatter x1, waiting for transfers between devices, local(): lax.psum_scatter(jnp.dot(full_acts, merged, preferred_element_type=jnp.fl...  42.9 us
    ppermute x3, waiting for transfers between devices, local(): terms = [lax.ppermute(terms[0], 'col', forward), *terms]  28 us
    dot_general x1, matrix products, local(): lax.dot_general(asq, gsq, (((0,), (0,)), ((), ())), preferred_element_typ...  10.4 us
  transfers between devices with their start and end apart: 8, of which 8 were waited for; matrix products, arithmetic and copies ran while one was open for 0% of the time, Pallas kernels for 0%

profile of v1, /device:TPU:8, one launch (start us, length us, event | category | flops | bytes accessed | tf_op | source)
XLA Modules:
  0.0 472.3 jit_solution(18210717580032254319)
XLA Ops:
  7.2 0.0 copy-start
  7.2 0.0 copy-start.2
  7.2 0.0 all-reduce.2.cloned.1.call-start
  7.2 1.7 collective-permute-start
  8.9 10.5 %collective-permute-done = bf16[128,1728]{0,1:T(8,128)(2,1)S(1)} collective-permute-done((bf16[128,1728]{0,1:T(8,128)(2,1)}, bf16[128,1728]{0,1:T(8,128)(2,1)S(1)}, u32[]{:S(2)}, u32[]{:S(2)}) %collective-permute-start) | collective-permute-done | bytes 442400 | tf_op jit(solution)/shard_map/ppermute | solution.py:24
  19.4 1.6 collective-permute-start.1
  21.0 9.3 %collective-permute-done.1 = bf16[128,1728]{0,1:T(8,128)(2,1)S(1)} collective-permute-done((bf16[128,1728]{0,1:T(8,128)(2,1)S(1)}, bf16[128,1728]{0,1:T(8,128)(2,1)S(1)}, u32[]{:S(2)}, u32[]{:S(2)}) %collective-permute-start.1) | collective-permute-done | bytes 442400 | tf_op jit(solution)/shard_map/ppermute | solution.py:24
  30.3 1.8 collective-permute-start.2
  32.0 0.0 copy-start.1
  32.0 8.2 %collective-permute-done.2 = bf16[128,1728]{0,1:T(8,128)(2,1)S(1)} collective-permute-done((bf16[128,1728]{0,1:T(8,128)(2,1)S(1)}, bf16[128,1728]{0,1:T(8,128)(2,1)S(1)}, u32[]{:S(2)}, u32[]{:S(2)}) %collective-permute-start.2) | collective-permute-done | bytes 442400 | tf_op jit(solution)/shard_map/ppermute | solution.py:24
  40.2 0.1 constant_dynamic-update-slice_fusion.7
  40.3 0.1 constant_dynamic-update-slice_fusion.6
  40.5 0.1 constant_dynamic-update-slice_fusion.5
  40.6 1.2 constant_dynamic-update-slice_fusion.4
  41.8 0.1 constant_dynamic-update-slice_fusion.3
  42.0 0.1 constant_dynamic-update-slice_fusion.2
  42.1 0.1 constant_dynamic-update-slice_fusion.1
  42.3 0.0 copy-done.2
  42.3 0.1 constant_dynamic-update-slice_fusion
  42.4 0.0 copy-start.3
  42.5 1.8 copy-done.3
  44.2 0.0 copy-done.1
  44.2 0.0 copy-start.4
  44.2 3.8 fusion.4
  48.0 0.0 all-reduce.2.cloned.1.call-update
  48.1 0.0 reduce-scatter.4.cloned.1.call-start
  48.1 92.9 %all-reduce.2.cloned.1.call-done = bf16[512,1280]{1,0:T(8,128)(2,1)} async-done(((bf16[512,1280]{1,0:T(8,128)(2,1)}), bf16[512,1280]{1,0:T(8,128)(2,1)}) %all-reduce.2.cloned.1.call-update) | async-done | bytes 1310736 | tf_op jit(solution)/shard_map/psum | solution.py:29
  141.0 0.0 copy-done
  141.0 0.0 copy-done.4
  141.0 10.4 %convert_multiply_fusion = (f32[1728,1280]{1,0:T(8,128)}, f32[1728,1280]{1,0:T(8,128)}) fusion(bf16[1,1728,1280]{2,1,0:T(8,128)(2,1)} %param.5, bf16[512,1280]{1,0:T(8,128)(2,1)} %all-reduce.2.cloned.1.call-done, bf16[1,128,1280]{2,1,0:T(8,128)(2,1)S(1)} %copy-done, s32[512]{0:T(512)S(1)} %bitcast.19, bf16[1024,1728]{0,1:T(8,128)(2,1)} %copy-done.3, ...), kind=kOutput, calls=%fused_computation | convolution fusion | flops 2442461184 | bytes 25528324 | tf_op jit(solution)/shard_map/dot_general | solution.py:34
  151.4 0.0 reduce-scatter.4.cloned.1.call-update
  151.4 0.0 reduce-scatter.6.cloned.1.call-start
  151.5 0.7 reduce-scatter.6.cloned.1.call-update
  152.2 0.0 all-gather.2.cloned.1.call-start
  152.2 96.2 %reduce-scatter.4.cloned.1.call-done = f32[216,1280]{1,0:T(8,128)} async-done(((f32[1728,1280]{1,0:T(8,128)}), f32[216,1280]{1,0:T(8,128)}) %reduce-scatter.4.cloned.1.call-update) | async-done | bytes 1105936 | tf_op jit(solution)/shard_map/reduce_scatter | solution.py:37
  248.4 103.5 %reduce-scatter.6.cloned.1.call-done = f32[216,1280]{1,0:T(8,128)} async-done(((f32[1728,1280]{1,0:T(8,128)}), f32[216,1280]{1,0:T(8,128)}) %reduce-scatter.6.cloned.1.call-update) | async-done | bytes 1105936 | tf_op jit(solution)/shard_map/reduce_scatter | solution.py:38
  351.9 2.6 divide_convert_fusion
  354.4 0.0 all-gather.2.cloned.1.call-update
  354.4 0.0 reduce-scatter.8.cloned.1.call-start
  354.5 57.2 %all-gather.2.cloned.1.call-done = bf16[1728,1280]{1,0:T(8,128)(2,1)} async-done(((bf16[216,1280]{1,0:T(8,128)(2,1)}), bf16[1728,1280]{1,0:T(8,128)(2,1)}) %all-gather.2.cloned.1.call-update) | async-done | bytes 4423696 | tf_op jit(solution)/shard_map/all_gather | solution.py:41
  411.7 6.5 %convolution_convert_fusion = bf16[512,1280]{1,0:T(8,128)(2,1)} fusion(bf16[1728,1280]{1,0:T(8,128)(2,1)} %all-gather.2.cloned.1.call-done, bf16[1024,1728]{0,1:T(8,128)(2,1)} %copy-done.3, s32[]{:T(128)S(6)} %select_n.14), kind=kOutput, calls=%fused_computation.8 | convolution fusion | flops 2265579520 | bytes 7503876 | tf_op jit(solution)/shard_map/dot_general | solution.py:43
  418.2 0.0 reduce-scatter.8.cloned.1.call-update
  418.2 42.9 %reduce-scatter.8.cloned.1.call-done = bf16[64,1280]{1,0:T(8,128)(2,1)} async-done(((bf16[512,1280]{1,0:T(8,128)(2,1)}), bf16[64,1280]{1,0:T(8,128)(2,1)}) %reduce-scatter.8.cloned.1.call-update) | async-done | bytes 163856 | tf_op jit(solution)/shard_map/reduce_scatter | solution.py:42
  461.1 4.6 copy.15
Async XLA Ops:
  7.2 133.9 %copy-start = (bf16[1,128,1280]{2,1,0:T(8,128)(2,1)S(1)}, bf16[1,128,1280]{2,1,0:T(8,128)(2,1)}, u32[]{:S(2)}) copy-start(bf16[1,128,1280]{2,1,0:T(8,128)(2,1)} %param.7) | copy-start | bytes 983044
  7.2 35.1 %copy-start.2 = (bf16[1,128,1728]{1,2,0:T(8,128)(2,1)S(1)}, bf16[1,128,1728]{1,2,0:T(8,128)(2,1)}, u32[]{:S(2)}) copy-start(bf16[1,128,1728]{1,2,0:T(8,128)(2,1)} %param.4) | copy-start | bytes 1327108
  7.2 133.8 %all-reduce.2.cloned.1.call-start = ((), (), s32[]{:S(2)}) async-start(), calls=%async_computation.3 | async-start | bytes 2621440 | tf_op jit(solution)/shard_map/psum | solution.py:29
  7.2 12.2 %collective-permute-start = (bf16[128,1728]{0,1:T(8,128)(2,1)}, bf16[128,1728]{0,1:T(8,128)(2,1)S(1)}, u32[]{:S(2)}, u32[]{:S(2)}) collective-permute-start(bf16[128,1728]{0,1:T(8,128)(2,1)} %bitcast.18), channel_id=1, source_target_pairs={{0,1},{1,2},{2,3},{3,0},{4,5},{5,6},{6,7},{7,4},{8,9},{9,10},{10,1... | collective-permute-start | bytes 1327112 | tf_op jit(solution)/shard_map/ppermute | solution.py:24
  19.4 10.8 %collective-permute-start.1 = (bf16[128,1728]{0,1:T(8,128)(2,1)S(1)}, bf16[128,1728]{0,1:T(8,128)(2,1)S(1)}, u32[]{:S(2)}, u32[]{:S(2)}) collective-permute-start(bf16[128,1728]{0,1:T(8,128)(2,1)S(1)} %collective-permute-done), channel_id=1, source_target_pairs={{0,1},{1,2},{2,3},{3,0},{4,5},{5,6},{6,7},{7,4},{8,9},{9,10},{10,1... | collective-permute-start | bytes 1327112 | tf_op jit(solution)/shard_map/ppermute | solution.py:24
  30.3 9.9 %collective-permute-start.2 = (bf16[128,1728]{0,1:T(8,128)(2,1)S(1)}, bf16[128,1728]{0,1:T(8,128)(2,1)S(1)}, u32[]{:S(2)}, u32[]{:S(2)}) collective-permute-start(bf16[128,1728]{0,1:T(8,128)(2,1)S(1)} %collective-permute-done.1), channel_id=1, source_target_pairs={{0,1},{1,2},{2,3},{3,0},{4,5},{5,6},{6,7},{7,4},{8,9},{9,10},{10,1... | collective-permute-start | bytes 1327112 | tf_op jit(solution)/shard_map/ppermute | solution.py:24
  32.0 12.2 %copy-start.1 = (bf16[1,1728,1280]{2,1,0:T(8,128)(2,1)S(1)}, bf16[1,1728,1280]{2,1,0:T(8,128)(2,1)}, u32[]{:S(2)}) copy-start(bf16[1,1728,1280]{2,1,0:T(8,128)(2,1)} %param.5) | copy-start | bytes 13271044
  42.4 1.8 copy-start.3
  44.2 96.8 %copy-start.4 = (s32[1,512]{1,0:T(1,128)S(1)}, s32[1,512]{1,0:T(1,128)}, u32[]{:S(2)}) copy-start(s32[1,512]{1,0:T(1,128)} %param.6) | copy-start | bytes 6148
  48.1 200.3 %reduce-scatter.4.cloned.1.call-start = ((), (), s32[]{:S(2)}) async-start(), calls=%async_computation.4 | async-start | bytes 9953280 | tf_op jit(solution)/shard_map/reduce_scatter | solution.py:37
  151.4 200.4 %reduce-scatter.6.cloned.1.call-start = ((), (), s32[]{:S(2)}) async-start(), calls=%async_computation.5 | async-start | bytes 9953280 | tf_op jit(solution)/shard_map/reduce_scatter | solution.py:38
  152.2 259.5 %all-gather.2.cloned.1.call-start = ((), (), s32[]{:S(2)}) async-start(), calls=%async_computation.6 | async-start | bytes 4976640 | tf_op jit(solution)/shard_map/all_gather | solution.py:41
  354.4 106.7 %reduce-scatter.8.cloned.1.call-start = ((), (), s32[]{:S(2)}) async-start(), calls=%async_computation.7 | async-start | bytes 1474560 | tf_op jit(solution)/shard_map/reduce_scatter | solution.py:42
Sparse Core Ops, SparseCore 0:
  48.2 92.8 all-reduce.1
  151.5 96.7 reduce-scatter.3
  251.1 100.6 reduce-scatter.5
  354.6 57.0 all-gather.1
  418.3 42.7 reduce-scatter.7
